TPU v7x, 256 devices: a whole 4x4x8 slice. The times are simulated.
256 devices in a mesh: section: 2 (over core), ctx: 32 (over z, x), mp: 4 (over y).
Axes of the slice: x: 4, y: 4, z: 8, core: 2. Of those that a mesh axis runs over, the one named last changes fastest.
Arguments:
- hidden: bfloat16 [2, 4096, 4672], P('section', 'ctx', 'mp'), may hold values from -120 to 120
- query: bfloat16 [2, 4096, 2048], P('section', 'ctx', 'mp'), may hold values from -6 to 6
- keys: bfloat16 [2, 4096, 2048], P('section', 'ctx', 'mp'), may hold values from -100 to 100
- values: bfloat16 [2, 4096, 2048], P('section', 'ctx', 'mp'), may hold values from -12 to 12
- w_out: bfloat16 [2, 4672, 2048], P('section', 'ctx', 'mp'), may hold values from -0.125 to 0.125
Outputs:
- handed: bfloat16 [2, 4096, 4672], P('section', 'ctx', 'mp')
- context: bfloat16 [2, 4096, 2048], P('section', 'ctx', 'mp')
All inputs are finite; a program needn't handle non-finite values.
Results may differ from a plain program's by a relative error of at most 0.0075.
Values may be sent and summed in bfloat16 or wider, within the bound.
No kernel may reach another device: no remote copies, remote signals or barrier semaphores. Data moves between devices by JAX's collectives and lax.ppermute only.
A program may use at most 128 MiB of HBM per device.

v0:
```python
import jax
import jax.numpy as jnp
from jax import lax
from jax.sharding import PartitionSpec as P

HEAD_DIM = 64


def from_behind(block, axis, distance):
    devices = range(lax.axis_size(axis))
    route = [((i - distance) % len(devices), i) for i in devices]
    return lax.ppermute(block, axis, route)


def head_scores(query_h, keys_h):
    return jnp.einsum("qd,kd->qk", query_h, keys_h, preferred_element_type=jnp.float32)


def body(hidden, query, keys, values, w_out):
    rows = hidden[0]
    query_rows = query[0]
    inner_dev = query_rows.shape[1]
    heads_dev = inner_dev // HEAD_DIM
    keys_local = keys[0]
    values_local = values[0]
    keys_all, values_all = (
        lax.all_gather(keys_local, "ctx", axis=0, tiled=True),
        lax.all_gather(values_local, "ctx", axis=0, tiled=True),
    )
    pieces = []
    for head in range(heads_dev):
        lower = head * HEAD_DIM
        upper = lower + HEAD_DIM
        scores = head_scores(query_rows[:, lower:upper], keys_all[:, lower:upper])
        peak = jnp.max(scores, axis=1, keepdims=True)
        expo = jnp.exp(scores - peak)
        total = jnp.sum(expo, axis=1, keepdims=True)
        summed = jnp.dot(
            expo.astype(jnp.bfloat16),
            values_all[:, lower:upper],
            preferred_element_type=jnp.float32,
        )
        pieces.append(summed / total)
    context = jnp.concatenate(pieces, axis=1).astype(jnp.bfloat16)
    out_local = w_out[0]
    branch_terms = jnp.einsum(
        "ri,di->rd",
        context,
        lax.all_gather(out_local, "ctx", axis=0, tiled=True),
        preferred_element_type=jnp.float32,
    )
    branch = lax.psum_scatter(
        branch_terms.astype(jnp.bfloat16), "mp", scatter_dimension=1, tiled=True
    ).astype(jnp.float32)
    result = (rows.astype(jnp.float32) + branch).astype(jnp.bfloat16)
    handed = from_behind(result, "section", 1)
    return (handed[None], context[None])


def solution(mesh):
    in_specs = (
        P("section", "ctx", "mp"),
        P("section", "ctx", "mp"),
        P("section", "ctx", "mp"),
        P("section", "ctx", "mp"),
        P("section", "ctx", "mp"),
    )
    out_specs = (P("section", "ctx", "mp"), P("section", "ctx", "mp"))
    return jax.shard_map(body, mesh=mesh, in_specs=in_specs, out_specs=out_specs, check_vma=False)
```

profile of v0, /device:TPU:1, one launch (start us, length us, event | category | flops | bytes accessed | tf_op | source)
XLA Modules:
  0.0 321.6 jit_solution(12413351099440571113)
XLA Ops:
  8.7 1.9 copy.10
  10.6 82.0 %all-gather.7.cloned.1.call-done = bf16[1,4096,512]{2,1,0:T(8,128)(2,1)} async-done(((bf16[1,128,512]{2,1,0:T(8,128)(2,1)}), bf16[1,4096,512]{2,1,0:T(8,128)(2,1)}) %all-gather.7.cloned.1.call-update) | async-done | bytes 4194320 | tf_op jit(solution)/shard_map/all_gather | solution.py:27
  92.6 1.8 fusion.75
  94.4 1.3 copy-done.12
  96.1 1.9 fusion.76
  98.0 1.3 copy-done.10
  99.8 1.8 fusion.77
  101.6 1.4 copy-done.8
  103.3 1.9 fusion.78
  105.2 1.4 copy-done.6
  107.0 1.8 fusion.79
  108.8 1.3 copy-done.4
  110.6 1.9 fusion.80
  112.5 1.4 copy-done.2
  114.3 1.8 fusion.81
  116.5 2.2 fusion.82
  119.2 54.6 %all-gather.9.cloned.1.call-done = bf16[1,4096,512]{2,1,0:T(8,128)(2,1)} async-done(((bf16[1,128,512]{2,1,0:T(8,128)(2,1)}), bf16[1,4096,512]{2,1,0:T(8,128)(2,1)}) %all-gather.9.cloned.1.call-update) | async-done | bytes 4194320 | tf_op jit(solution)/shard_map/all_gather | solution.py:28
  173.7 2.6 constant_dynamic-update-slice_fusion.7
  176.4 2.4 constant_dynamic-update-slice_fusion.6
  178.8 2.0 constant_dynamic-update-slice_fusion.5
  180.9 2.4 constant_dynamic-update-slice_fusion.4
  183.3 2.0 constant_dynamic-update-slice_fusion.3
  185.4 2.4 constant_dynamic-update-slice_fusion.2
  187.8 1.9 constant_dynamic-update-slice_fusion.1
  189.7 2.5 constant_dynamic-update-slice_fusion
  192.2 88.1 %all-gather.11.cloned.1.call-done = bf16[1,4672,512]{2,0,1:T(2,128)(2,1)} async-done(((bf16[1,146,512]{2,0,1:T(2,128)(2,1)}), bf16[1,4672,512]{2,0,1:T(2,128)(2,1)}) %all-gather.11.cloned.1.call-update) | async-done | bytes 4784144 | tf_op jit(solution)/shard_map/all_gather | solution.py:49
  280.3 6.2 %convolution_convert_fusion = bf16[128,4672]{0,1:T(8,128)(2,1)} fusion(bf16[128,512]{0,1:T(8,128)(2,1)S(1)} %get-tuple-element.38, bf16[1,4672,512]{2,0,1:T(2,128)(2,1)} %all-gather.11.cloned.1.call-done), kind=kOutput, calls=%fused_computation | convolution fusion | flops 612966400 | bytes 6111232 | tf_op jit(solution)/shard_map/ri,di->rd/dot_general | solution.py:46
  286.6 23.2 %reduce-scatter.2.cloned.1.call-done = bf16[128,1168]{0,1:T(8,128)(2,1)} async-done(((bf16[128,4672]{0,1:T(8,128)(2,1)}), bf16[128,1168]{0,1:T(8,128)(2,1)}) %reduce-scatter.2.cloned.1.call-update) | async-done | bytes 299024 | tf_op jit(solution)/shard_map/reduce_scatter | solution.py:52
  309.8 1.0 fusion.66
  310.8 2.3 collective-permute-start
  313.2 0.8 copy.11
  314.4 0.7 copy.32
  (47 shorter events, 5.6 us)
Async XLA Ops:
  7.2 85.4 %all-gather.7.cloned.1.call-start = ((), (), s32[]{:S(2)}) async-start(), calls=%async_computation.2 | async-start | bytes 4325376 | tf_op jit(solution)/shard_map/all_gather | solution.py:27
  7.9 165.8 %all-gather.9.cloned.1.call-start = ((), (), s32[]{:S(2)}) async-start(), calls=%async_computation.3 | async-start | bytes 4325376 | tf_op jit(solution)/shard_map/all_gather | solution.py:28
  8.6 271.6 %all-gather.11.cloned.1.call-start = ((), (), s32[]{:S(2)}) async-start(), calls=%async_computation.4 | async-start | bytes 9867264 | tf_op jit(solution)/shard_map/all_gather | solution.py:49
  10.6 299.2 %reduce-scatter.2.cloned.1.call-start = ((), (), s32[]{:S(2)}) async-start(), calls=%async_computation.1 | async-start | bytes 1495040 | tf_op jit(solution)/shard_map/reduce_scatter | solution.py:52
  94.4 1.3 copy-start.12
  98.0 1.4 copy-start.10
  101.6 1.4 copy-start.8
  105.2 1.4 copy-start.6
  108.8 1.3 copy-start.4
  112.5 1.4 copy-start.2
  116.1 2.6 copy-start
  173.7 2.6 copy-start.11
  176.4 2.5 copy-start.9
  178.8 2.0 copy-start.7
  180.8 2.5 copy-start.5
  183.3 2.0 copy-start.3
  185.3 2.5 copy-start.1
  280.3 29.5 %copy-start.13 = (bf16[1,128,1168]{1,2,0:T(8,128)(2,1)S(1)}, bf16[1,128,1168]{1,2,0:T(8,128)(2,1)}, u32[]{:S(2)}) copy-start(bf16[1,128,1168]{1,2,0:T(8,128)(2,1)} %param.5) | copy-start | bytes 897028
  310.8 3.6 %collective-permute-start = (bf16[128,1168]{0,1:T(8,128)(2,1)S(1)}, bf16[128,1168]{0,1:T(8,128)(2,1)S(1)}, u32[]{:S(2)}, u32[]{:S(2)}) collective-permute-start(bf16[128,1168]{0,1:T(8,128)(2,1)S(1)} %fusion.66), channel_id=1, source_target_pairs={{128,0},{0,128},{129,1},{1,129},{130,2},{2,130},{131,3},{3,131},{1... | collective-permute-start | bytes 897032 | tf_op jit(solution)/shard_map/ppermute | solution.py:12
Sparse Core Ops, SparseCore 0:
  10.6 81.9 all-gather.6
  95.2 78.5 all-gather.8
  176.9 103.3 all-gather.10
  286.6 23.1 reduce-scatter.1
where the time goes:
time: 322 us
  waiting for transfers between devices  250 us (78%)
  matrix products  39.4 us (12%)
  between operations  14 us (4%)
  local copies, waits for them, and re-layouts  11.6 us (4%)
  other arithmetic  4.54 us (1%)
    all_gather x1, waiting for transfers between devices, body(): lax.all_gather(out_local, 'ctx', axis=0, tiled=True)  88.1 us
    all_gather x1, waiting for transfers between devices, body(): lax.all_gather(keys_local, 'ctx', axis=0, tiled=True)  82 us
    all_gather x1, waiting for transfers between devices, body(): lax.all_gather(values_local, 'ctx', axis=0, tiled=True)  54.6 us
    reduce_scatter x1, waiting for transfers between devices, body(): lax.psum_scatter(branch_terms.astype(jnp.bfloat16), 'mp', scatter_dimensi...  23.2 us
    dot_general x8, matrix products, body(): jnp.dot(expo.astype(jnp.bfloat16), values_all[:, lower:upper], preferred_...  18.3 us
    dot_general x8, matrix products, head_scores(): jnp.einsum('qd,kd->qk', query_h, keys_h, preferred_element_type=jnp.float32)  14.9 us
    unnamed x38, local copies, waits for them, and re-layouts  11.6 us
  transfers between devices with their start and end apart: 5, of which 5 were waited for; matrix products, arithmetic and copies ran while one was open for 12% of the time, Pallas kernels for 0%

commit v1 on v0

--- a/solution.py
+++ b/solution.py
@@ -4,6 +4,11 @@
 from jax.sharding import PartitionSpec as P
 
 HEAD_DIM = 64
+
+
+def swapped_in(array, axis, dim):
+    repeated = jnp.stack([array] * lax.axis_size(axis))
+    return jnp.concatenate(lax.all_to_all(repeated, axis, 0, 0), axis=dim)
 
 
 def from_behind(block, axis, distance):
@@ -24,7 +29,7 @@
     keys_local = keys[0]
     values_local = values[0]
     keys_all, values_all = (
-        lax.all_gather(keys_local, "ctx", axis=0, tiled=True),
+        swapped_in(keys_local, "ctx", 0),
         lax.all_gather(values_local, "ctx", axis=0, tiled=True),
     )
     pieces = []

time: 322 us -> 289 us (0.90)
  waiting for transfers between devices: 250 us -> 202 us
  starting transfers between devices: 2.5 us -> 14.6 us
    all_to_all x0 -> x1, waiting for transfers between devices: none -> 117 us  [swapped_in(): return jnp.concatenate(lax.all_to_all(repeated, axis, 0, 0), axis=dim)]
    all_gather x1 -> x0, waiting for transfers between devices: 82 us -> none  [body(): lax.all_gather(keys_local, 'ctx', axis=0, tiled=True)]
    all_gather x1, waiting for transfers between devices: 54.6 us -> 0.02 us  [body(): lax.all_gather(values_local, 'ctx', axis=0, tiled=True)]
    all_gather x1, waiting for transfers between devices: 88.1 us -> 61.3 us  [body(): lax.all_gather(out_local, 'ctx', axis=0, tiled=True)]
    all_to_all x0 -> x1, starting transfers between devices: none -> 12.1 us  [swapped_in(): return jnp.concatenate(lax.all_to_all(repeated, axis, 0, 0), axis=dim)]
    another operation x0 -> x1, local copies, waits for them, and re-layouts: none -> 3.37 us  [swapped_in(): repeated = jnp.stack([array] * lax.axis_size(axis))]
    unnamed x38 -> x40, local copies, waits for them, and re-layouts: 11.6 us -> 10.7 us
  transfers between devices with their start and end apart: 5 -> 5, of which waited for: 5 -> 4; matrix products, arithmetic and copies ran while one was open for 12% -> 14% of each run, Pallas kernels for 0% -> 0%
where the time goes in v1:
time: 289 us
  waiting for transfers between devices  202 us (70%)
  matrix products  39.4 us (14%)
  starting transfers between devices  14.6 us (5%)
  local copies, waits for them, and re-layouts  14 us (5%)
  between operations  14 us (5%)
  other arithmetic  4.54 us (2%)
    all_to_all x1, waiting for transfers between devices, swapped_in(): return jnp.concatenate(lax.all_to_all(repeated, axis, 0, 0), axis=dim)  117 us
    all_gather x1, waiting for transfers between devices, body(): lax.all_gather(out_local, 'ctx', axis=0, tiled=True)  61.3 us
    reduce_scatter x1, waiting for transfers between devices, body(): lax.psum_scatter(branch_terms.astype(jnp.bfloat16), 'mp', scatter_dimensi...  23.2 us
    dot_general x8, matrix products, body(): jnp.dot(expo.astype(jnp.bfloat16), values_all[:, lower:upper], preferred_...  18.3 us
    dot_general x8, matrix products, head_scores(): jnp.einsum('qd,kd->qk', query_h, keys_h, preferred_element_type=jnp.float32)  14.9 us
    all_to_all x1, starting transfers between devices, swapped_in(): return jnp.concatenate(lax.all_to_all(repeated, axis, 0, 0), axis=dim)  12.1 us
    unnamed x40, local copies, waits for them, and re-layouts  10.7 us
    dot_general x1, matrix products, body(): jnp.einsum('ri,di->rd', context, lax.all_gather(out_local, 'ctx', axis=0,...  6.19 us
  transfers between devices with their start and end apart: 5, of which 4 were waited for; matrix products, arithmetic and copies ran while one was open for 14% of the time, Pallas kernels for 0%

profile of v1, /device:TPU:1, one launch (start us, length us, event | category | flops | bytes accessed | tf_op | source)
XLA Modules:
  0.0 289.0 jit_solution(15524089712625017005)
XLA Ops:
  7.9 3.4 %stack.3 = bf16[32,128,512]{2,1,0:T(8,128)(2,1)} broadcast(bf16[128,512]{1,0:T(8,128)(2,1)} %bitcast.45), dimensions={1,2} | broadcast | bytes 4325376 | tf_op jit(solution)/shard_map/stack | solution.py:10
  11.3 12.1 %all-to-all-start = ((bf16[32,128,512]{2,1,0:T(8,128)(2,1)}), bf16[32,128,512]{2,1,0:T(8,128)(2,1)}, u32[]{:S(2)}, u32[]{:S(2)}) async-start(bf16[32,128,512]{2,1,0:T(8,128)(2,1)} %stack.3), calls=%async_computation | async-start | bytes 8388608 | tf_op jit(solution)/shard_map/all_to_all | solution.py:11
  23.5 0.9 copy.10
  24.5 116.7 %all-to-all-done = bf16[32,128,512]{2,1,0:T(8,128)(2,1)} async-done(((bf16[32,128,512]{2,1,0:T(8,128)(2,1)}), bf16[32,128,512]{2,1,0:T(8,128)(2,1)}, u32[]{:S(2)}, u32[]{:S(2)}) %all-to-all-start) | async-done | bytes 4194336 | tf_op jit(solution)/shard_map/all_to_all | solution.py:11
  141.2 1.8 fusion.75
  142.9 1.3 copy-done.12
  144.7 1.9 fusion.76
  146.6 1.3 copy-done.10
  148.4 1.8 fusion.77
  150.1 1.4 copy-done.8
  151.9 1.9 fusion.78
  153.8 1.4 copy-done.6
  155.6 1.8 fusion.79
  157.4 1.3 copy-done.4
  159.2 1.9 fusion.80
  161.1 1.4 copy-done.2
  162.9 1.8 fusion.81
  165.2 2.1 fusion.82
  167.8 2.6 constant_dynamic-update-slice_fusion.7
  170.5 2.4 constant_dynamic-update-slice_fusion.6
  172.9 2.0 constant_dynamic-update-slice_fusion.5
  175.0 2.4 constant_dynamic-update-slice_fusion.4
  177.4 2.0 constant_dynamic-update-slice_fusion.3
  179.5 2.4 constant_dynamic-update-slice_fusion.2
  181.9 1.9 constant_dynamic-update-slice_fusion.1
  183.8 2.5 constant_dynamic-update-slice_fusion
  186.3 61.3 %all-gather.7.cloned.1.call-done = bf16[1,4672,512]{2,0,1:T(2,128)(2,1)} async-done(((bf16[1,146,512]{2,0,1:T(2,128)(2,1)}), bf16[1,4672,512]{2,0,1:T(2,128)(2,1)}) %all-gather.7.cloned.1.call-update) | async-done | bytes 4784144 | tf_op jit(solution)/shard_map/all_gather | solution.py:54
  247.6 6.2 %convolution_convert_fusion = bf16[128,4672]{0,1:T(8,128)(2,1)} fusion(bf16[128,512]{0,1:T(8,128)(2,1)S(1)} %get-tuple-element.38, bf16[1,4672,512]{2,0,1:T(2,128)(2,1)} %all-gather.7.cloned.1.call-done), kind=kOutput, calls=%fused_computation | convolution fusion | flops 612966400 | bytes 6111232 | tf_op jit(solution)/shard_map/ri,di->rd/dot_general | solution.py:51
  253.9 23.2 %reduce-scatter.2.cloned.1.call-done = bf16[128,1168]{0,1:T(8,128)(2,1)} async-done(((bf16[128,4672]{0,1:T(8,128)(2,1)}), bf16[128,1168]{0,1:T(8,128)(2,1)}) %reduce-scatter.2.cloned.1.call-update) | async-done | bytes 299024 | tf_op jit(solution)/shard_map/reduce_scatter | solution.py:57
  277.1 1.0 fusion.66
  278.1 2.4 collective-permute-start
  280.5 0.8 copy.11
  (49 shorter events, 5.6 us)
Async XLA Ops:
  7.2 160.6 %all-gather.5.cloned.1.call-start = ((), (), s32[]{:S(2)}) async-start(), calls=%async_computation.3 | async-start | bytes 4325376 | tf_op jit(solution)/shard_map/all_gather | solution.py:33
  11.3 12.2 %copy-start.14 = (bf16[1,146,512]{2,1,0:T(8,128)(2,1)S(1)}, bf16[1,146,512]{2,1,0:T(8,128)(2,1)}, u32[]{:S(2)}) copy-start(bf16[1,146,512]{2,1,0:T(8,128)(2,1)} %param.9) | copy-start | bytes 448516
  11.3 129.9 %all-to-all-start = ((bf16[32,128,512]{2,1,0:T(8,128)(2,1)}), bf16[32,128,512]{2,1,0:T(8,128)(2,1)}, u32[]{:S(2)}, u32[]{:S(2)}) async-start(bf16[32,128,512]{2,1,0:T(8,128)(2,1)} %stack.3), calls=%async_computation | async-start | bytes 8388608 | tf_op jit(solution)/shard_map/all_to_all | solution.py:11
  23.4 224.2 %all-gather.7.cloned.1.call-start = ((), (), s32[]{:S(2)}) async-start(), calls=%async_computation.4 | async-start | bytes 9867264 | tf_op jit(solution)/shard_map/all_gather | solution.py:54
  24.4 252.7 %reduce-scatter.2.cloned.1.call-start = ((), (), s32[]{:S(2)}) async-start(), calls=%async_computation.2 | async-start | bytes 1495040 | tf_op jit(solution)/shard_map/reduce_scatter | solution.py:57
  142.9 1.3 copy-start.12
  146.6 1.4 copy-start.10
  150.1 1.4 copy-start.8
  153.8 1.4 copy-start.6
  157.4 1.3 copy-start.4
  161.1 1.4 copy-start.2
  164.7 2.6 copy-start
  167.8 2.7 copy-start.11
  170.4 2.5 copy-start.9
  172.9 2.0 copy-start.7
  174.9 2.5 copy-start.5
  177.4 2.1 copy-start.3
  179.5 2.5 copy-start.1
  247.6 29.5 %copy-start.13 = (bf16[1,128,1168]{1,2,0:T(8,128)(2,1)S(1)}, bf16[1,128,1168]{1,2,0:T(8,128)(2,1)}, u32[]{:S(2)}) copy-start(bf16[1,128,1168]{1,2,0:T(8,128)(2,1)} %param.5) | copy-start | bytes 897028
  278.1 3.6 %collective-permute-start = (bf16[128,1168]{0,1:T(8,128)(2,1)S(1)}, bf16[128,1168]{0,1:T(8,128)(2,1)S(1)}, u32[]{:S(2)}, u32[]{:S(2)}) collective-permute-start(bf16[128,1168]{0,1:T(8,128)(2,1)S(1)} %fusion.66), channel_id=1, source_target_pairs={{128,0},{0,128},{129,1},{1,129},{130,2},{2,130},{131,3},{3,131},{1... | collective-permute-start | bytes 897032 | tf_op jit(solution)/shard_map/ppermute | solution.py:17
Sparse Core Ops, SparseCore 0:
  10.6 127.7 all-gather.4
  141.5 105.9 all-gather.6
  253.9 23.1 reduce-scatter.1
